TPU v7x, 32 devices: a whole 2x2x4 slice. The times are simulated.
32 devices in a mesh: groups: 2 (over y), shots: 4 (over z), dom: 2 (over x), sub: 2 (over core).
Axes of the slice: x: 2, y: 2, z: 4, core: 2. Of those that a mesh axis runs over, the one named last changes fastest.
Arguments:
- velocity: float32 [64, 16, 256], P(('groups', 'shots'), 'dom', 'sub'), parts along dimension 0, may hold values from 0.15 to 0.4
- wave_prev: bfloat16 [8, 32, 16, 256], P(('groups', 'shots'), None, 'dom', 'sub'), parts along dimension 0, may hold values from -6 to 6
- wave_now: bfloat16 [8, 32, 16, 256], P(('groups', 'shots'), None, 'dom', 'sub'), parts along dimension 0, may hold values from -6 to 6
- adj_next: bfloat16 [8, 32, 16, 256], P(('groups', 'shots'), None, 'dom', 'sub'), parts along dimension 0, may hold values from -6 to 6
- adj_now: bfloat16 [8, 32, 16, 256], P(('groups', 'shots'), None, 'dom', 'sub'), parts along dimension 0, may hold values from -6 to 6
- sponge: int32 [32, 16, 256], P(None, 'dom', 'sub'), may hold values 0 or 1
- wavelet: float32 [8, 6], P(('groups', 'shots')), parts along dimension 0, may hold values from -12 to 12
- src_pos: int32 [8], P(('groups', 'shots')), parts along dimension 0, may hold values from 0 to 4095
- rec_pos: int32 [8, 256], P(('groups', 'shots')), parts along dimension 0, may hold values from 0 to 4095
- observed: float32 [8, 4, 256], P(('groups', 'shots')), parts along dimension 0, may hold values from -6 to 6
Outputs:
- direction: float32 [64, 16, 256], P(('groups', 'shots'), 'dom', 'sub'), parts along dimension 0
- wave_out: float32 [8, 32, 16, 256], P(('groups', 'shots'), None, 'dom', 'sub'), parts along dimension 0
There are 2 independent parts, one for each index of `groups`. A program takes and returns all parts, laid end to end along the dimension named above; an argument that names none is the same for every part. Nothing has to cross between parts.
Inputs may be any that keep to these rules, and one draw needn't show every extreme that they name: `src_pos`: a horizontal position x * 256 + y on the grid. `rec_pos`: horizontal positions x * 256 + y on the grid, possibly repeated.
All inputs are finite; a program needn't handle non-finite values. Where the computation divides by a largest or mean magnitude, that divisor is 1e-20 or more. No bound on the sum of `sponge` on one device may be relied on, other than what follows from the above.
Results may differ from a plain program's by a relative error of at most 0.0003.
Values sent between devices are 32-bit elements; how exact they have to be, the bound alone decides.
A program may use at most 64 MiB of HBM per device.

v0:
```python
import jax
import jax.numpy as jnp
from jax import lax
from jax.sharding import PartitionSpec as P

NF = 4
NFIN = 2
coeffs = (-205.0 / 72.0, 8.0 / 5.0, -1.0 / 5.0, 8.0 / 315.0, -1.0 / 560.0)
damp_rate = 0.2
step_rate = 0.1
floor_share = 0.5
src_depth = 2
rec_depth = 1
reach = 4


def padded_2(cells, sides, width):
    for axis, dim in sides:
        count = lax.axis_size(axis)
        ends = count - 1
        head = lax.slice_in_dim(cells, 0, width, axis=dim)
        tail = lax.slice_in_dim(cells, cells.shape[dim] - width, cells.shape[dim], axis=dim)
        cells = jnp.concatenate(
            [
                lax.ppermute(tail, axis, [(i, (i + 1) % count) for i in range(ends)]),
                cells,
                lax.ppermute(head, axis, [((i + 1) % count, i) for i in range(ends)]),
            ],
            axis=dim,
        )
    return cells


def laplace(padded, depth, rows, cols):
    z0, x0, y0 = (reach, reach, reach)
    total = 3.0 * coeffs[0] * padded[z0 : z0 + depth, x0 : x0 + rows, y0 : y0 + cols]
    for offset in range(1, 5):
        pair = padded[z0 + offset : z0 + offset + depth, x0 : x0 + rows, y0 : y0 + cols]
        pair = pair + padded[z0 - offset : z0 - offset + depth, x0 : x0 + rows, y0 : y0 + cols]
        pair = pair + padded[z0 : z0 + depth, x0 + offset : x0 + offset + rows, y0 : y0 + cols]
        pair = pair + padded[z0 : z0 + depth, x0 - offset : x0 - offset + rows, y0 : y0 + cols]
        pair = pair + padded[z0 : z0 + depth, x0 : x0 + rows, y0 + offset : y0 + offset + cols]
        pair = pair + padded[z0 : z0 + depth, x0 : x0 + rows, y0 - offset : y0 - offset + cols]
        total = total + coeffs[offset] * pair
    return total


def advance(now, before, kappa, damp, plane, level):
    widened = padded_2(now, (("dom", 1), ("sub", 2)), 4)
    padded = jnp.pad(widened, ((reach, reach), (0, 0), (0, 0)))
    lap = laplace(padded, now.shape[0], now.shape[1], now.shape[2])
    numer = 2.0 * now - (1.0 - damp) * before + kappa * lap
    numer = numer.at[level].add(plane)
    return numer / (1.0 + damp)


def local_spots(positions, rows, cols):
    cols_all = cols * lax.axis_size("sub")
    gx = positions // cols_all
    gy = positions % cols_all
    local_x = gx - lax.axis_index("dom") * rows
    local_y = gy - lax.axis_index("sub") * cols
    inside = (local_x >= 0) & (local_x < rows) & (local_y >= 0) & (local_y < cols)
    spots = jnp.where(inside, local_x * cols + local_y, 0)
    return (spots, inside)


def place_local(spots, inside, values, rows, cols):
    kept = jnp.where(inside, values, 0.0)
    flat = jnp.zeros((rows * cols,), jnp.float32).at[spots].add(kept)
    return flat.reshape(rows, cols)


def shards(
    velocity, wave_prev, wave_now, adj_next, adj_now, sponge, wavelet, src_pos, rec_pos, observed
):
    depth, rows, cols = sponge.shape
    full_vel = lax.all_gather(velocity, "shots", axis=0, tiled=True)
    kappa = full_vel * full_vel
    damp = damp_rate * sponge.astype(jnp.float32)
    amps = wavelet[0]
    src_spot, src_inside = local_spots(src_pos, rows, cols)
    rec_spot, rec_inside = local_spots(rec_pos[0], rows, cols)
    states = [wave_prev[0].astype(jnp.float32), wave_now[0].astype(jnp.float32)]
    for step in range(NF):
        plane = place_local(src_spot, src_inside, amps[step][None], rows, cols)
        states.append(advance(states[-1], states[-2], kappa, damp, plane, src_depth))
    lam_after = adj_next[0].astype(jnp.float32)
    lam_now = adj_now[0].astype(jnp.float32)
    grad = jnp.zeros_like(kappa)
    for level in range(NF, 0, -1):
        sampled = states[level + 1][rec_depth].reshape(-1)[rec_spot]
        resid = sampled - observed[0, level - 1]
        plane = place_local(rec_spot, rec_inside, resid, rows, cols)
        lam_before = advance(lam_now, lam_after, kappa, damp, plane, rec_depth)
        lower = level - 1
        accel = states[lower + 2] - 2.0 * states[lower + 1] + states[lower]
        grad = grad + lam_before * accel
        lam_after, lam_now = (lam_now, lam_before)
    illum = jnp.zeros_like(kappa)
    for level in range(1, NF + 1):
        illum = illum + states[level + 1] * states[level + 1]
    shot_count = lax.axis_size("shots")
    grad_all, illum_all = lax.psum((grad, illum), "shots")
    precond = grad_all / (illum_all + floor_share * shot_count)
    peak = lax.pmax(jnp.max(jnp.abs(precond)), ("dom", "sub"))
    full_dir = precond / (peak + 1e-06)
    updated = full_vel * (1.0 - step_rate * full_dir)
    owned = velocity.shape[0]
    direction = lax.dynamic_slice_in_dim(full_dir, lax.axis_index("shots") * owned, owned, 0)
    kappa_new = updated * updated
    before, current = (states[-2], states[-1])
    for step in range(NFIN):
        plane = place_local(src_spot, src_inside, amps[NF + step][None], rows, cols)
        following = advance(current, before, kappa_new, damp, plane, src_depth)
        before, current = (current, following)
    return (direction, current[None])


def solution(mesh):
    return jax.shard_map(
        shards,
        mesh=mesh,
        in_specs=(
            P(("groups", "shots"), "dom", "sub"),
            P(("groups", "shots"), None, "dom", "sub"),
            P(("groups", "shots"), None, "dom", "sub"),
            P(("groups", "shots"), None, "dom", "sub"),
            P(("groups", "shots"), None, "dom", "sub"),
            P(None, "dom", "sub"),
            P(("groups", "shots"), None),
            P(("groups", "shots")),
            P(("groups", "shots"), None),
            P(("groups", "shots"), None, None),
        ),
        out_specs=(
            P(("groups", "shots"), "dom", "sub"),
            P(("groups", "shots"), None, "dom", "sub"),
        ),
        check_vma=False,
    )
```

profile of v0, /device:TPU:0, one launch (start us, length us, event | category | flops | bytes accessed | tf_op | source)
XLA Modules:
  0.0 231.8 jit_solution(6835556315163786703)
XLA Ops:
  8.1 4.9 %collective-permute-start.4 = (f32[32,4,128]{2,1,0:T(4,128)S(1)}, f32[32,4,128]{2,1,0:T(4,128)S(1)}, u32[]{:S(2)}, u32[]{:S(2)}) collective-permute-start(f32[32,4,128]{2,1,0:T(4,128)S(1)} %get-tuple-element.261), channel_id=1, source_target_pairs={{0,2},{1,3},{4,6},{5,7},{8,10},{9,11},{12,14},{13,15},{16,18},{17,... | collective-permute-start | bytes 196616 | tf_op jit(solution)/shard_map/ppermute | solution.py:25
  14.3 4.5 %collective-permute-start = (f32[32,4,128]{2,1,0:T(4,128)S(1)}, f32[32,4,128]{2,1,0:T(4,128)S(1)}, u32[]{:S(2)}, u32[]{:S(2)}) collective-permute-start(f32[32,4,128]{2,1,0:T(4,128)S(1)} %get-tuple-element.251), channel_id=1, source_target_pairs={{0,2},{1,3},{4,6},{5,7},{8,10},{9,11},{12,14},{13,15},{16,18},{17,... | collective-permute-start | bytes 196616 | tf_op jit(solution)/shard_map/ppermute | solution.py:25
  27.0 2.6 %fusion.344 = f32[1024]{0:T(1024)S(1)} fusion(f32[1024]{0:T(1024)S(1)} %broadcast.395.clone, s32[]{:T(128)} %bitcast.12, pred[1]{0:T(512)(128)(4,1)} %get-tuple-element.275, f32[1,1]{1,0:T(1,128)} %get-tuple-element.270, s32[1]{0:T(128)} %compare_select_fusion.1), kind=kLoop, calls=%fused_computation.685 | loop fusion | flops 5 | bytes 525 | tf_op jit(solution)/shard_map/scatter-add | solution.py:70
  29.6 2.6 %fusion.342 = f32[1024]{0:T(1024)S(1)} fusion(f32[1024]{0:T(1024)S(1)} %broadcast.395.clone.1, s32[]{:T(128)} %bitcast.12, pred[1]{0:T(512)(128)(4,1)} %get-tuple-element.275, f32[1,1]{1,0:T(1,128)} %get-tuple-element.269, s32[1]{0:T(128)} %compare_select_fusion.1), kind=kLoop, calls=%fused_computation.682 | loop fusion | flops 5 | bytes 525 | tf_op jit(solution)/shard_map/scatter-add | solution.py:70
  32.3 2.6 %fusion.340 = f32[1024]{0:T(1024)S(1)} fusion(f32[1024]{0:T(1024)S(1)} %broadcast.395.clone.2, s32[]{:T(128)} %bitcast.12, pred[1]{0:T(512)(128)(4,1)} %get-tuple-element.275, f32[1,1]{1,0:T(1,128)} %get-tuple-element.268, s32[1]{0:T(128)} %compare_select_fusion.1), kind=kLoop, calls=%fused_computation.679 | loop fusion | flops 5 | bytes 525 | tf_op jit(solution)/shard_map/scatter-add | solution.py:70
  34.9 2.6 %fusion.338 = f32[1024]{0:T(1024)S(1)} fusion(f32[1024]{0:T(1024)S(1)} %broadcast.395.clone.3, s32[]{:T(128)} %bitcast.12, pred[1]{0:T(512)(128)(4,1)} %get-tuple-element.275, f32[1,1]{1,0:T(1,128)} %get-tuple-element.267, s32[1]{0:T(128)} %compare_select_fusion.1), kind=kLoop, calls=%fused_computation.676 | loop fusion | flops 5 | bytes 525 | tf_op jit(solution)/shard_map/scatter-add | solution.py:70
  37.5 13.6 %all_gather.3 = f32[32,8,128]{2,1,0:T(8,128)S(1)} all-gather(f32[8,8,128]{2,1,0:T(8,128)S(1)} %copy-done.7), channel_id=1, replica_groups=mesh['groups'=2,'shots'=4,'dom'=2,'sub'=2] {'shots'}, dimensions={0}, use_global_device_ids=true | all-gather | bytes 163840 | tf_op jit(solution)/shard_map/all_gather | solution.py:78
  54.1 3.1 %collective-permute-start.2 = (f32[32,16,4]{2,1,0:T(8,128)S(1)}, f32[32,16,4]{2,1,0:T(8,128)S(1)}, u32[]{:S(2)}, u32[]{:S(2)}) collective-permute-start(f32[32,16,4]{2,1,0:T(8,128)S(1)} %get-tuple-element.221), channel_id=1, source_target_pairs={{0,1},{2,3},{4,5},{6,7},{8,9},{10,11},{12,13},{14,15},{16,17},{18,... | collective-permute-start | bytes 24584 | tf_op jit(solution)/shard_map/ppermute | solution.py:25
  60.5 4.5 %collective-permute-start.8 = (f32[32,4,128]{2,1,0:T(4,128)S(1)}, f32[32,4,128]{2,1,0:T(4,128)S(1)}, u32[]{:S(2)}, u32[]{:S(2)}) collective-permute-start(f32[32,4,128]{2,1,0:T(4,128)S(1)} %get-tuple-element.259), channel_id=1, source_target_pairs={{0,2},{1,3},{4,6},{5,7},{8,10},{9,11},{12,14},{13,15},{16,18},{17,... | collective-permute-start | bytes 196616 | tf_op jit(solution)/shard_map/ppermute | solution.py:25
  67.3 4.5 %collective-permute-done.9 = f32[32,4,128]{2,1,0:T(4,128)S(1)} collective-permute-done((f32[32,4,128]{2,1,0:T(4,128)S(1)}, f32[32,4,128]{2,1,0:T(4,128)S(1)}, u32[]{:S(2)}, u32[]{:S(2)}) %collective-permute-start.9) | collective-permute-done | bytes 65568 | tf_op jit(solution)/shard_map/ppermute | solution.py:27
  83.0 3.5 %collective-permute-done.13 = f32[32,4,128]{2,1,0:T(4,128)S(1)} collective-permute-done((f32[32,4,128]{2,1,0:T(4,128)S(1)}, f32[32,4,128]{2,1,0:T(4,128)S(1)}, u32[]{:S(2)}, u32[]{:S(2)}) %collective-permute-start.13) | collective-permute-done | bytes 65568 | tf_op jit(solution)/shard_map/ppermute | solution.py:27
  97.1 3.5 %collective-permute-done.17 = f32[32,4,128]{2,1,0:T(4,128)S(1)} collective-permute-done((f32[32,4,128]{2,1,0:T(4,128)S(1)}, f32[32,4,128]{2,1,0:T(4,128)S(1)}, u32[]{:S(2)}, u32[]{:S(2)}) %collective-permute-start.17) | collective-permute-done | bytes 65568 | tf_op jit(solution)/shard_map/ppermute | solution.py:27
  109.0 2.3 %scatter_custom_fusion = f32[1024]{0:T(1024)S(1)} fusion(s32[256]{0:T(256)S(1)} %bitcast.109, f32[256]{0:T(256)S(1)} %get-tuple-element.274, f32[]{:T(128)} %constant.405.clone.1), kind=kCustom, calls=%fused_computation.646 | custom fusion | flops 256 | bytes 4100 | tf_op jit(solution)/shard_map/scatter-add | solution.py:70
  115.1 4.1 %collective-permute-done.21 = f32[32,4,128]{2,1,0:T(4,128)S(1)} collective-permute-done((f32[32,4,128]{2,1,0:T(4,128)S(1)}, f32[32,4,128]{2,1,0:T(4,128)S(1)}, u32[]{:S(2)}, u32[]{:S(2)}) %collective-permute-start.21) | collective-permute-done | bytes 65568 | tf_op jit(solution)/shard_map/ppermute | solution.py:27
  122.1 2.3 %scatter_custom_fusion.1 = f32[1024]{0:T(1024)S(1)} fusion(s32[256]{0:T(256)S(1)} %bitcast.110, f32[256]{0:T(256)S(1)} %get-tuple-element.273, f32[]{:T(128)} %constant.405.clone.1), kind=kCustom, calls=%fused_computation.644 | custom fusion | flops 256 | bytes 4100 | tf_op jit(solution)/shard_map/scatter-add | solution.py:70
  129.7 4.5 %collective-permute-done.25 = f32[32,4,128]{2,1,0:T(4,128)S(1)} collective-permute-done((f32[32,4,128]{2,1,0:T(4,128)S(1)}, f32[32,4,128]{2,1,0:T(4,128)S(1)}, u32[]{:S(2)}, u32[]{:S(2)}) %collective-permute-start.25) | collective-permute-done | bytes 65568 | tf_op jit(solution)/shard_map/ppermute | solution.py:27
  140.0 2.3 %scatter_custom_fusion.2 = f32[1024]{0:T(1024)S(1)} fusion(s32[256]{0:T(256)S(1)} %bitcast.112, f32[256]{0:T(256)S(1)} %get-tuple-element.272, f32[]{:T(128)} %constant.405.clone.1), kind=kCustom, calls=%fused_computation.642 | custom fusion | flops 256 | bytes 4100 | tf_op jit(solution)/shard_map/scatter-add | solution.py:70
  146.6 4.5 %collective-permute-start.32 = (f32[32,4,128]{2,1,0:T(4,128)S(1)}, f32[32,4,128]{2,1,0:T(4,128)S(1)}, u32[]{:S(2)}, u32[]{:S(2)}) collective-permute-start(f32[32,4,128]{2,1,0:T(4,128)S(1)} %get-tuple-element.253), channel_id=1, source_target_pairs={{0,2},{1,3},{4,6},{5,7},{8,10},{9,11},{12,14},{13,15},{16,18},{17,... | collective-permute-start | bytes 196616 | tf_op jit(solution)/shard_map/ppermute | solution.py:25
  152.7 2.3 %collective-permute-start.30 = (f32[32,16,4]{2,1,0:T(8,128)S(1)}, f32[32,16,4]{2,1,0:T(8,128)S(1)}, u32[]{:S(2)}, u32[]{:S(2)}) collective-permute-start(f32[32,16,4]{2,1,0:T(8,128)S(1)} %get-tuple-element.209), channel_id=1, source_target_pairs={{0,1},{2,3},{4,5},{6,7},{8,9},{10,11},{12,13},{14,15},{16,17},{18,... | collective-permute-start | bytes 24584 | tf_op jit(solution)/shard_map/ppermute | solution.py:25
  164.2 2.6 %fusion.336 = f32[1024]{0:T(1024)S(1)} fusion(f32[1024]{0:T(1024)S(1)} %broadcast.395.clone.4, s32[]{:T(128)} %bitcast.12, pred[1]{0:T(512)(128)(4,1)} %get-tuple-element.275, f32[1,1]{1,0:T(1,128)} %get-tuple-element.271, s32[1]{0:T(128)} %compare_select_fusion.1), kind=kLoop, calls=%fused_computation.673 | loop fusion | flops 5 | bytes 525 | tf_op jit(solution)/shard_map/scatter-add | solution.py:70
  167.1 31.3 %all-reduce.13.cloned.1.call-done = (f32[32,8,128]{2,1,0:T(8,128)}, f32[32,8,128]{2,1,0:T(8,128)}) async-done(((f32[32,8,128]{2,1,0:T(8,128)}, f32[32,8,128]{2,1,0:T(8,128)}), (f32[32,8,128]{2,1,0:T(8,128)}, f32[32,8,128]{2,1,0:T(8,128)})) %all-reduce.13.cloned.1.call-update) | async-done | bytes 262160 | tf_op jit(solution)/shard_map/psum | solution.py:104
  200.4 6.3 %pmax.7 = f32[]{:T(128)} all-reduce(f32[]{:T(128)} %abs_reduce_fusion), channel_id=1, replica_groups=mesh['groups'=2,'shots'=4,'dom'=2,'sub'=2] {'dom','sub'}, use_global_device_ids=true, to_apply=%region_7.8 | all-reduce | flops 1 | bytes 8 | tf_op jit(solution)/shard_map/pmax | solution.py:106
  208.1 3.6 %collective-permute-start.36 = (f32[32,4,128]{2,1,0:T(4,128)S(1)}, f32[32,4,128]{2,1,0:T(4,128)S(1)}, u32[]{:S(2)}, u32[]{:S(2)}) collective-permute-start(f32[32,4,128]{2,1,0:T(4,128)S(1)} %get-tuple-element.243), channel_id=1, source_target_pairs={{0,2},{1,3},{4,6},{5,7},{8,10},{9,11},{12,14},{13,15},{16,18},{17,... | collective-permute-start | bytes 196616 | tf_op jit(solution)/shard_map/ppermute | solution.py:25
  213.1 2.6 %fusion.334 = f32[1024]{0:T(1024)S(1)} fusion(f32[1024]{0:T(1024)S(1)} %broadcast.395.clone.5, s32[]{:T(128)} %bitcast.12, pred[1]{0:T(512)(128)(4,1)} %get-tuple-element.275, f32[1,1]{1,0:T(1,128)} %get-tuple-element.266, s32[1]{0:T(128)} %compare_select_fusion.1), kind=kLoop, calls=%fused_computation.670 | loop fusion | flops 5 | bytes 525 | tf_op jit(solution)/shard_map/scatter-add | solution.py:70
  (198 shorter events, 90.9 us)
Async XLA Ops:
  7.2 191.2 %all-reduce.13.cloned.1.call-start = ((), (), s32[]{:S(2)}) async-start(), calls=%async_computation | async-start | bytes 524288 | tf_op jit(solution)/shard_map/psum | solution.py:104
  8.1 43.0 %collective-permute-start.4 = (f32[32,4,128]{2,1,0:T(4,128)S(1)}, f32[32,4,128]{2,1,0:T(4,128)S(1)}, u32[]{:S(2)}, u32[]{:S(2)}) collective-permute-start(f32[32,4,128]{2,1,0:T(4,128)S(1)} %get-tuple-element.261), channel_id=1, source_target_pairs={{0,2},{1,3},{4,6},{5,7},{8,10},{9,11},{12,14},{13,15},{16,18},{17,... | collective-permute-start | bytes 196616 | tf_op jit(solution)/shard_map/ppermute | solution.py:25
  13.0 38.1 %collective-permute-start.5 = (f32[32,4,128]{2,1,0:T(4,128)S(1)}, f32[32,4,128]{2,1,0:T(4,128)S(1)}, u32[]{:S(2)}, u32[]{:S(2)}) collective-permute-start(f32[32,4,128]{2,1,0:T(4,128)S(1)} %get-tuple-element.260), channel_id=1, source_target_pairs={{2,0},{3,1},{6,4},{7,5},{10,8},{11,9},{14,12},{15,13},{18,16},{19,... | collective-permute-start | bytes 196616 | tf_op jit(solution)/shard_map/ppermute | solution.py:27
  14.3 39.5 %collective-permute-start = (f32[32,4,128]{2,1,0:T(4,128)S(1)}, f32[32,4,128]{2,1,0:T(4,128)S(1)}, u32[]{:S(2)}, u32[]{:S(2)}) collective-permute-start(f32[32,4,128]{2,1,0:T(4,128)S(1)} %get-tuple-element.251), channel_id=1, source_target_pairs={{0,2},{1,3},{4,6},{5,7},{8,10},{9,11},{12,14},{13,15},{16,18},{17,... | collective-permute-start | bytes 196616 | tf_op jit(solution)/shard_map/ppermute | solution.py:25
  18.9 35.0 %collective-permute-start.1 = (f32[32,4,128]{2,1,0:T(4,128)S(1)}, f32[32,4,128]{2,1,0:T(4,128)S(1)}, u32[]{:S(2)}, u32[]{:S(2)}) collective-permute-start(f32[32,4,128]{2,1,0:T(4,128)S(1)} %get-tuple-element.250), channel_id=1, source_target_pairs={{2,0},{3,1},{6,4},{7,5},{10,8},{11,9},{14,12},{15,13},{18,16},{19,... | collective-permute-start | bytes 196616 | tf_op jit(solution)/shard_map/ppermute | solution.py:27
  51.3 7.2 %collective-permute-start.6 = (f32[32,16,4]{2,1,0:T(8,128)S(1)}, f32[32,16,4]{2,1,0:T(8,128)S(1)}, u32[]{:S(2)}, u32[]{:S(2)}) collective-permute-start(f32[32,16,4]{2,1,0:T(8,128)S(1)} %get-tuple-element.241), channel_id=1, source_target_pairs={{0,1},{2,3},{4,5},{6,7},{8,9},{10,11},{12,13},{14,15},{16,17},{18,... | collective-permute-start | bytes 24584 | tf_op jit(solution)/shard_map/ppermute | solution.py:25
  52.6 5.9 %collective-permute-start.7 = (f32[32,16,4]{2,1,0:T(8,128)S(1)}, f32[32,16,4]{2,1,0:T(8,128)S(1)}, u32[]{:S(2)}, u32[]{:S(2)}) collective-permute-start(f32[32,16,4]{2,1,0:T(8,128)S(1)} %get-tuple-element.240), channel_id=1, source_target_pairs={{1,0},{3,2},{5,4},{7,6},{9,8},{11,10},{13,12},{15,14},{17,16},{19,... | collective-permute-start | bytes 24584 | tf_op jit(solution)/shard_map/ppermute | solution.py:27
  54.1 12.2 %collective-permute-start.2 = (f32[32,16,4]{2,1,0:T(8,128)S(1)}, f32[32,16,4]{2,1,0:T(8,128)S(1)}, u32[]{:S(2)}, u32[]{:S(2)}) collective-permute-start(f32[32,16,4]{2,1,0:T(8,128)S(1)} %get-tuple-element.221), channel_id=1, source_target_pairs={{0,1},{2,3},{4,5},{6,7},{8,9},{10,11},{12,13},{14,15},{16,17},{18,... | collective-permute-start | bytes 24584 | tf_op jit(solution)/shard_map/ppermute | solution.py:25
  57.2 9.2 %collective-permute-start.3 = (f32[32,16,4]{2,1,0:T(8,128)S(1)}, f32[32,16,4]{2,1,0:T(8,128)S(1)}, u32[]{:S(2)}, u32[]{:S(2)}) collective-permute-start(f32[32,16,4]{2,1,0:T(8,128)S(1)} %get-tuple-element.220), channel_id=1, source_target_pairs={{1,0},{3,2},{5,4},{7,6},{9,8},{11,10},{13,12},{15,14},{17,16},{19,... | collective-permute-start | bytes 24584 | tf_op jit(solution)/shard_map/ppermute | solution.py:27
  60.5 6.9 %collective-permute-start.8 = (f32[32,4,128]{2,1,0:T(4,128)S(1)}, f32[32,4,128]{2,1,0:T(4,128)S(1)}, u32[]{:S(2)}, u32[]{:S(2)}) collective-permute-start(f32[32,4,128]{2,1,0:T(4,128)S(1)} %get-tuple-element.259), channel_id=1, source_target_pairs={{0,2},{1,3},{4,6},{5,7},{8,10},{9,11},{12,14},{13,15},{16,18},{17,... | collective-permute-start | bytes 196616 | tf_op jit(solution)/shard_map/ppermute | solution.py:25
  65.0 6.7 %collective-permute-start.9 = (f32[32,4,128]{2,1,0:T(4,128)S(1)}, f32[32,4,128]{2,1,0:T(4,128)S(1)}, u32[]{:S(2)}, u32[]{:S(2)}) collective-permute-start(f32[32,4,128]{2,1,0:T(4,128)S(1)} %get-tuple-element.258), channel_id=1, source_target_pairs={{2,0},{3,1},{6,4},{7,5},{10,8},{11,9},{14,12},{15,13},{18,16},{19,... | collective-permute-start | bytes 196616 | tf_op jit(solution)/shard_map/ppermute | solution.py:27
  80.3 6.2 %collective-permute-start.13 = (f32[32,4,128]{2,1,0:T(4,128)S(1)}, f32[32,4,128]{2,1,0:T(4,128)S(1)}, u32[]{:S(2)}, u32[]{:S(2)}) collective-permute-start(f32[32,4,128]{2,1,0:T(4,128)S(1)} %get-tuple-element.256), channel_id=1, source_target_pairs={{2,0},{3,1},{6,4},{7,5},{10,8},{11,9},{14,12},{15,13},{18,16},{19,... | collective-permute-start | bytes 196616 | tf_op jit(solution)/shard_map/ppermute | solution.py:27
  94.4 6.2 %collective-permute-start.17 = (f32[32,4,128]{2,1,0:T(4,128)S(1)}, f32[32,4,128]{2,1,0:T(4,128)S(1)}, u32[]{:S(2)}, u32[]{:S(2)}) collective-permute-start(f32[32,4,128]{2,1,0:T(4,128)S(1)} %get-tuple-element.254), channel_id=1, source_target_pairs={{2,0},{3,1},{6,4},{7,5},{10,8},{11,9},{14,12},{15,13},{18,16},{19,... | collective-permute-start | bytes 196616 | tf_op jit(solution)/shard_map/ppermute | solution.py:27
  113.0 6.2 %collective-permute-start.21 = (f32[32,4,128]{2,1,0:T(4,128)S(1)}, f32[32,4,128]{2,1,0:T(4,128)S(1)}, u32[]{:S(2)}, u32[]{:S(2)}) collective-permute-start(f32[32,4,128]{2,1,0:T(4,128)S(1)} %get-tuple-element.248), channel_id=1, source_target_pairs={{2,0},{3,1},{6,4},{7,5},{10,8},{11,9},{14,12},{15,13},{18,16},{19,... | collective-permute-start | bytes 196616 | tf_op jit(solution)/shard_map/ppermute | solution.py:27
  127.4 6.8 %collective-permute-start.25 = (f32[32,4,128]{2,1,0:T(4,128)S(1)}, f32[32,4,128]{2,1,0:T(4,128)S(1)}, u32[]{:S(2)}, u32[]{:S(2)}) collective-permute-start(f32[32,4,128]{2,1,0:T(4,128)S(1)} %get-tuple-element.246), channel_id=1, source_target_pairs={{2,0},{3,1},{6,4},{7,5},{10,8},{11,9},{14,12},{15,13},{18,16},{19,... | collective-permute-start | bytes 196616 | tf_op jit(solution)/shard_map/ppermute | solution.py:27
  134.4 7.9 %collective-permute-start.26 = (f32[32,16,4]{2,1,0:T(8,128)S(1)}, f32[32,16,4]{2,1,0:T(8,128)S(1)}, u32[]{:S(2)}, u32[]{:S(2)}) collective-permute-start(f32[32,16,4]{2,1,0:T(8,128)S(1)} %get-tuple-element.213), channel_id=1, source_target_pairs={{0,1},{2,3},{4,5},{6,7},{8,9},{10,11},{12,13},{14,15},{16,17},{18,... | collective-permute-start | bytes 24584 | tf_op jit(solution)/shard_map/ppermute | solution.py:25
  136.4 6.0 %collective-permute-start.27 = (f32[32,16,4]{2,1,0:T(8,128)S(1)}, f32[32,16,4]{2,1,0:T(8,128)S(1)}, u32[]{:S(2)}, u32[]{:S(2)}) collective-permute-start(f32[32,16,4]{2,1,0:T(8,128)S(1)} %get-tuple-element.212), channel_id=1, source_target_pairs={{1,0},{3,2},{5,4},{7,6},{9,8},{11,10},{13,12},{15,14},{17,16},{19,... | collective-permute-start | bytes 24584 | tf_op jit(solution)/shard_map/ppermute | solution.py:27
  143.8 8.7 %collective-permute-start.28 = (f32[32,4,128]{2,1,0:T(4,128)S(1)}, f32[32,4,128]{2,1,0:T(4,128)S(1)}, u32[]{:S(2)}, u32[]{:S(2)}) collective-permute-start(f32[32,4,128]{2,1,0:T(4,128)S(1)} %get-tuple-element.245), channel_id=1, source_target_pairs={{0,2},{1,3},{4,6},{5,7},{8,10},{9,11},{12,14},{13,15},{16,18},{17,... | collective-permute-start | bytes 196616 | tf_op jit(solution)/shard_map/ppermute | solution.py:25
  145.3 7.2 %collective-permute-start.29 = (f32[32,4,128]{2,1,0:T(4,128)S(1)}, f32[32,4,128]{2,1,0:T(4,128)S(1)}, u32[]{:S(2)}, u32[]{:S(2)}) collective-permute-start(f32[32,4,128]{2,1,0:T(4,128)S(1)} %get-tuple-element.244), channel_id=1, source_target_pairs={{2,0},{3,1},{6,4},{7,5},{10,8},{11,9},{14,12},{15,13},{18,16},{19,... | collective-permute-start | bytes 196616 | tf_op jit(solution)/shard_map/ppermute | solution.py:27
  146.6 9.9 %collective-permute-start.32 = (f32[32,4,128]{2,1,0:T(4,128)S(1)}, f32[32,4,128]{2,1,0:T(4,128)S(1)}, u32[]{:S(2)}, u32[]{:S(2)}) collective-permute-start(f32[32,4,128]{2,1,0:T(4,128)S(1)} %get-tuple-element.253), channel_id=1, source_target_pairs={{0,2},{1,3},{4,6},{5,7},{8,10},{9,11},{12,14},{13,15},{16,18},{17,... | collective-permute-start | bytes 196616 | tf_op jit(solution)/shard_map/ppermute | solution.py:25
  151.2 6.3 %collective-permute-start.33 = (f32[32,4,128]{2,1,0:T(4,128)S(1)}, f32[32,4,128]{2,1,0:T(4,128)S(1)}, u32[]{:S(2)}, u32[]{:S(2)}) collective-permute-start(f32[32,4,128]{2,1,0:T(4,128)S(1)} %get-tuple-element.252), channel_id=1, source_target_pairs={{2,0},{3,1},{6,4},{7,5},{10,8},{11,9},{14,12},{15,13},{18,16},{19,... | collective-permute-start | bytes 196616 | tf_op jit(solution)/shard_map/ppermute | solution.py:27
  160.8 5.9 %collective-permute-start.34 = (f32[32,16,4]{2,1,0:T(8,128)S(1)}, f32[32,16,4]{2,1,0:T(8,128)S(1)}, u32[]{:S(2)}, u32[]{:S(2)}) collective-permute-start(f32[32,16,4]{2,1,0:T(8,128)S(1)} %get-tuple-element.225), channel_id=1, source_target_pairs={{0,1},{2,3},{4,5},{6,7},{8,9},{10,11},{12,13},{14,15},{16,17},{18,... | collective-permute-start | bytes 24584 | tf_op jit(solution)/shard_map/ppermute | solution.py:25
  208.1 7.6 %collective-permute-start.36 = (f32[32,4,128]{2,1,0:T(4,128)S(1)}, f32[32,4,128]{2,1,0:T(4,128)S(1)}, u32[]{:S(2)}, u32[]{:S(2)}) collective-permute-start(f32[32,4,128]{2,1,0:T(4,128)S(1)} %get-tuple-element.243), channel_id=1, source_target_pairs={{0,2},{1,3},{4,6},{5,7},{8,10},{9,11},{12,14},{13,15},{16,18},{17,... | collective-permute-start | bytes 196616 | tf_op jit(solution)/shard_map/ppermute | solution.py:25
  211.8 6.2 %collective-permute-start.37 = (f32[32,4,128]{2,1,0:T(4,128)S(1)}, f32[32,4,128]{2,1,0:T(4,128)S(1)}, u32[]{:S(2)}, u32[]{:S(2)}) collective-permute-start(f32[32,4,128]{2,1,0:T(4,128)S(1)} %get-tuple-element.242), channel_id=1, source_target_pairs={{2,0},{3,1},{6,4},{7,5},{10,8},{11,9},{14,12},{15,13},{18,16},{19,... | collective-permute-start | bytes 196616 | tf_op jit(solution)/shard_map/ppermute | solution.py:27
  (28 other events, 109.3 us)
Sparse Core Ops, SparseCore 0:
  160.8 37.5 all-reduce.12
where the time goes:
time: 233 us; the launch traced here: 232 us
  starting transfers between devices  74 us (32%)
  waiting for transfers between devices  63 us (27%)
  other arithmetic  45.3 us (19%)
  blocking collectives  19.9 us (9%)
  between operations  19.5 us (8%)
  local copies, waits for them, and re-layouts  10.1 us (4%)
    ppermute x20, starting transfers between devices, padded_2(): lax.ppermute(tail, axis, [(i, (i + 1) % count) for i in range(ends)])  47.7 us
    psum x1, waiting for transfers between devices, shards(): grad_all, illum_all = lax.psum((grad, illum), 'shots')  31.3 us
    ppermute x20, waiting for transfers between devices, padded_2(): lax.ppermute(head, axis, [((i + 1) % count, i) for i in range(ends)])  29.7 us
    ppermute x20, starting transfers between devices, padded_2(): lax.ppermute(head, axis, [((i + 1) % count, i) for i in range(ends)])  26.2 us
    scatter-add x10, other arithmetic, place_local(): flat = jnp.zeros((rows * cols,), jnp.float32).at[spots].add(kept)  24.9 us
    all_gather x1, blocking collectives, shards(): full_vel = lax.all_gather(velocity, 'shots', axis=0, tiled=True)  13.6 us
    concatenate x30, other arithmetic, padded_2(): jnp.concatenate([lax.ppermute(tail, axis, [(i, (i + 1) % count) for i in...  8.09 us
    pmax x1, blocking collectives, shards(): peak = lax.pmax(jnp.max(jnp.abs(precond)), ('dom', 'sub'))  6.3 us
  transfers between devices with their start and end apart: 41, of which 16 were waited for; matrix products, arithmetic and copies ran while one was open for 14% of the time, Pallas kernels for 0%

commit v1 on v0

--- a/solution.py
+++ b/solution.py
@@ -1,3 +1,4 @@
+import functools
 import jax
 import jax.numpy as jnp
 from jax import lax
@@ -12,6 +13,31 @@
 src_depth = 2
 rec_depth = 1
 reach = 4
+
+
+def get_map_now(chunk, dim_i):
+    y_new = list(chunk.shape[1:])
+    y_new[dim_i] *= chunk.shape[0]
+    return jnp.moveaxis(chunk, 0, dim_i).reshape(y_new)
+
+
+def choose_halves_now(shard_in, bus_axis):
+    degree = lax.axis_size(bus_axis)
+    k_now = shard_in[None]
+    for j0 in range(degree.bit_length() - 1):
+        big = 1 << j0
+        z2 = lax.ppermute(k_now, bus_axis, perm=list(map(lambda pp: (pp, pp ^ big), range(degree))))
+        work_now = jnp.stack([k_now, z2], axis=0)
+        small = lax.axis_index(bus_axis) >> j0 & 1
+        k_now = jnp.where(small == 0, work_now, work_now[::-1]).reshape(-1, *shard_in.shape)
+    return k_now
+
+
+def view_the_plane(v0, vals, dim_at):
+    return get_map_now(choose_halves_now(v0, vals), dim_at)
+
+
+feed_samples_all = functools.partial(view_the_plane, vals="shots", dim_at=0)
 
 
 def padded_2(cells, sides, width):
@@ -75,7 +101,7 @@
     velocity, wave_prev, wave_now, adj_next, adj_now, sponge, wavelet, src_pos, rec_pos, observed
 ):
     depth, rows, cols = sponge.shape
-    full_vel = lax.all_gather(velocity, "shots", axis=0, tiled=True)
+    full_vel = feed_samples_all(velocity)
     kappa = full_vel * full_vel
     damp = damp_rate * sponge.astype(jnp.float32)
     amps = wavelet[0]

time: 233 us -> 223 us (0.957)
  blocking collectives: 19.9 us -> 6.3 us
  starting transfers between devices: 74 us -> 77.8 us
    all_gather x1 -> x0, blocking collectives: 13.6 us -> none  [shards(): full_vel = lax.all_gather(velocity, 'shots', axis=0, tiled=True)]
    ppermute x0 -> x2, starting transfers between devices: none -> 4.3 us  [choose_halves_now(): lax.ppermute(k_now, bus_axis, perm=list(map(lambda pp: (pp, pp ^ big), ra...]
    psum x1, waiting for transfers between devices: 31.3 us -> 28.4 us  [shards(): grad_all, illum_all = lax.psum((grad, illum), 'shots')]
  transfers between devices with their start and end apart: 41 -> 43, of which waited for: 16 -> 17; matrix products, arithmetic and copies ran while one was open for 14% -> 15% of each run, Pallas kernels for 0% -> 0%
where the time goes in v1:
time: 223 us; the launch traced here: 221 us
  starting transfers between devices  77.8 us (35%)
  waiting for transfers between devices  61.7 us (28%)
  other arithmetic  45.5 us (20%)
  between operations  19.6 us (9%)
  local copies, waits for them, and re-layouts  10.5 us (5%)
  blocking collectives  6.3 us (3%)
    ppermute x20, starting transfers between devices, padded_2(): lax.ppermute(tail, axis, [(i, (i + 1) % count) for i in range(ends)])  47.2 us
    ppermute x20, waiting for transfers between devices, padded_2(): lax.ppermute(head, axis, [((i + 1) % count, i) for i in range(ends)])  31.4 us
    psum x1, waiting for transfers between devices, shards(): grad_all, illum_all = lax.psum((grad, illum), 'shots')  28.4 us
    ppermute x20, starting transfers between devices, padded_2(): lax.ppermute(head, axis, [((i + 1) % count, i) for i in range(ends)])  26.2 us
    scatter-add x10, other arithmetic, place_local(): flat = jnp.zeros((rows * cols,), jnp.float32).at[spots].add(kept)  25.2 us
    concatenate x30, other arithmetic, padded_2(): jnp.concatenate([lax.ppermute(tail, axis, [(i, (i + 1) % count) for i in...  8.08 us
    pmax x1, blocking collectives, shards(): peak = lax.pmax(jnp.max(jnp.abs(precond)), ('dom', 'sub'))  6.3 us
    add x10, other arithmetic, advance(): numer = 2.0 * now - (1.0 - damp) * before + kappa * lap  5.95 us
  transfers between devices with their start and end apart: 43, of which 17 were waited for; matrix products, arithmetic and copies ran while one was open for 15% of the time, Pallas kernels for 0%

profile of v1, /device:TPU:0, one launch (start us, length us, event | category | flops | bytes accessed | tf_op | source)
XLA Modules:
  0.0 221.4 jit_solution(8008560285924287874)
XLA Ops:
  8.1 4.9 %collective-permute-start.6 = (f32[32,4,128]{2,1,0:T(4,128)S(1)}, f32[32,4,128]{2,1,0:T(4,128)S(1)}, u32[]{:S(2)}, u32[]{:S(2)}) collective-permute-start(f32[32,4,128]{2,1,0:T(4,128)S(1)} %get-tuple-element.261), channel_id=1, source_target_pairs={{0,2},{1,3},{4,6},{5,7},{8,10},{9,11},{12,14},{13,15},{16,18},{17,... | collective-permute-start | bytes 196616 | tf_op jit(solution)/shard_map/ppermute | solution.py:51
  16.0 4.5 %collective-permute-start.2 = (f32[32,4,128]{2,1,0:T(4,128)S(1)}, f32[32,4,128]{2,1,0:T(4,128)S(1)}, u32[]{:S(2)}, u32[]{:S(2)}) collective-permute-start(f32[32,4,128]{2,1,0:T(4,128)S(1)} %get-tuple-element.251), channel_id=1, source_target_pairs={{0,2},{1,3},{4,6},{5,7},{8,10},{9,11},{12,14},{13,15},{16,18},{17,... | collective-permute-start | bytes 196616 | tf_op jit(solution)/shard_map/ppermute | solution.py:51
  28.8 2.7 %fusion.347 = f32[1024]{0:T(1024)S(1)} fusion(f32[1024]{0:T(1024)S(1)} %broadcast.399.clone, s32[]{:T(128)} %bitcast.19, pred[1]{0:T(512)(128)(4,1)} %get-tuple-element.277, f32[1,1]{1,0:T(1,128)} %get-tuple-element.272, s32[1]{0:T(128)} %compare_select_fusion.1), kind=kLoop, calls=%fused_computation.693 | loop fusion | flops 5 | bytes 525 | tf_op jit(solution)/shard_map/scatter-add | solution.py:96
  31.6 2.6 %fusion.345 = f32[1024]{0:T(1024)S(1)} fusion(f32[1024]{0:T(1024)S(1)} %broadcast.399.clone.1, s32[]{:T(128)} %bitcast.19, pred[1]{0:T(512)(128)(4,1)} %get-tuple-element.277, f32[1,1]{1,0:T(1,128)} %get-tuple-element.271, s32[1]{0:T(128)} %compare_select_fusion.1), kind=kLoop, calls=%fused_computation.690 | loop fusion | flops 5 | bytes 525 | tf_op jit(solution)/shard_map/scatter-add | solution.py:96
  34.2 2.7 %fusion.343 = f32[1024]{0:T(1024)S(1)} fusion(f32[1024]{0:T(1024)S(1)} %broadcast.399.clone.2, s32[]{:T(128)} %bitcast.19, pred[1]{0:T(512)(128)(4,1)} %get-tuple-element.277, f32[1,1]{1,0:T(1,128)} %get-tuple-element.270, s32[1]{0:T(128)} %compare_select_fusion.1), kind=kLoop, calls=%fused_computation.687 | loop fusion | flops 5 | bytes 525 | tf_op jit(solution)/shard_map/scatter-add | solution.py:96
  36.9 2.6 %fusion.341 = f32[1024]{0:T(1024)S(1)} fusion(f32[1024]{0:T(1024)S(1)} %broadcast.399.clone.3, s32[]{:T(128)} %bitcast.19, pred[1]{0:T(512)(128)(4,1)} %get-tuple-element.277, f32[1,1]{1,0:T(1,128)} %get-tuple-element.269, s32[1]{0:T(128)} %compare_select_fusion.1), kind=kLoop, calls=%fused_computation.684 | loop fusion | flops 5 | bytes 525 | tf_op jit(solution)/shard_map/scatter-add | solution.py:96
  39.5 2.7 %collective-permute-start.1 = (f32[2,8,8,128]{3,2,1,0:T(8,128)S(1)}, f32[2,8,8,128]{3,2,1,0:T(8,128)S(1)}, u32[]{:S(2)}, u32[]{:S(2)}) collective-permute-start(f32[2,8,8,128]{3,2,1,0:T(8,128)S(1)} %get-tuple-element.263), channel_id=1, source_target_pairs={{0,8},{4,12},{8,0},{12,4},{1,9},{5,13},{9,1},{13,5},{2,10},{6,14},... | collective-permute-start | bytes 196616 | tf_op jit(solution)/shard_map/ppermute | solution.py:29
  45.2 3.1 %collective-permute-start.4 = (f32[32,16,4]{2,1,0:T(8,128)S(1)}, f32[32,16,4]{2,1,0:T(8,128)S(1)}, u32[]{:S(2)}, u32[]{:S(2)}) collective-permute-start(f32[32,16,4]{2,1,0:T(8,128)S(1)} %get-tuple-element.221), channel_id=1, source_target_pairs={{0,1},{2,3},{4,5},{6,7},{8,9},{10,11},{12,13},{14,15},{16,17},{18,... | collective-permute-start | bytes 24584 | tf_op jit(solution)/shard_map/ppermute | solution.py:51
  54.1 4.5 %collective-permute-start.10 = (f32[32,4,128]{2,1,0:T(4,128)S(1)}, f32[32,4,128]{2,1,0:T(4,128)S(1)}, u32[]{:S(2)}, u32[]{:S(2)}) collective-permute-start(f32[32,4,128]{2,1,0:T(4,128)S(1)} %get-tuple-element.259), channel_id=1, source_target_pairs={{0,2},{1,3},{4,6},{5,7},{8,10},{9,11},{12,14},{13,15},{16,18},{17,... | collective-permute-start | bytes 196616 | tf_op jit(solution)/shard_map/ppermute | solution.py:51
  60.6 4.3 %collective-permute-done.11 = f32[32,4,128]{2,1,0:T(4,128)S(1)} collective-permute-done((f32[32,4,128]{2,1,0:T(4,128)S(1)}, f32[32,4,128]{2,1,0:T(4,128)S(1)}, u32[]{:S(2)}, u32[]{:S(2)}) %collective-permute-start.11) | collective-permute-done | bytes 65568 | tf_op jit(solution)/shard_map/ppermute | solution.py:53
  75.5 3.5 %collective-permute-done.15 = f32[32,4,128]{2,1,0:T(4,128)S(1)} collective-permute-done((f32[32,4,128]{2,1,0:T(4,128)S(1)}, f32[32,4,128]{2,1,0:T(4,128)S(1)}, u32[]{:S(2)}, u32[]{:S(2)}) %collective-permute-start.15) | collective-permute-done | bytes 65568 | tf_op jit(solution)/shard_map/ppermute | solution.py:53
  89.7 3.5 %collective-permute-done.19 = f32[32,4,128]{2,1,0:T(4,128)S(1)} collective-permute-done((f32[32,4,128]{2,1,0:T(4,128)S(1)}, f32[32,4,128]{2,1,0:T(4,128)S(1)}, u32[]{:S(2)}, u32[]{:S(2)}) %collective-permute-start.19) | collective-permute-done | bytes 65568 | tf_op jit(solution)/shard_map/ppermute | solution.py:53
  101.6 2.3 %scatter_custom_fusion = f32[1024]{0:T(1024)S(1)} fusion(s32[256]{0:T(256)S(1)} %bitcast.146, f32[256]{0:T(256)S(1)} %get-tuple-element.276, f32[]{:T(128)} %constant.410.clone.1), kind=kCustom, calls=%fused_computation.654 | custom fusion | flops 256 | bytes 4100 | tf_op jit(solution)/shard_map/scatter-add | solution.py:96
  107.6 4.1 %collective-permute-done.23 = f32[32,4,128]{2,1,0:T(4,128)S(1)} collective-permute-done((f32[32,4,128]{2,1,0:T(4,128)S(1)}, f32[32,4,128]{2,1,0:T(4,128)S(1)}, u32[]{:S(2)}, u32[]{:S(2)}) %collective-permute-start.23) | collective-permute-done | bytes 65568 | tf_op jit(solution)/shard_map/ppermute | solution.py:53
  114.6 2.3 %scatter_custom_fusion.1 = f32[1024]{0:T(1024)S(1)} fusion(s32[256]{0:T(256)S(1)} %bitcast.147, f32[256]{0:T(256)S(1)} %get-tuple-element.275, f32[]{:T(128)} %constant.410.clone.1), kind=kCustom, calls=%fused_computation.652 | custom fusion | flops 256 | bytes 4100 | tf_op jit(solution)/shard_map/scatter-add | solution.py:96
  122.2 4.5 %collective-permute-done.27 = f32[32,4,128]{2,1,0:T(4,128)S(1)} collective-permute-done((f32[32,4,128]{2,1,0:T(4,128)S(1)}, f32[32,4,128]{2,1,0:T(4,128)S(1)}, u32[]{:S(2)}, u32[]{:S(2)}) %collective-permute-start.27) | collective-permute-done | bytes 65568 | tf_op jit(solution)/shard_map/ppermute | solution.py:53
  130.2 2.3 %scatter_custom_fusion.3 = f32[1024]{0:T(1024)S(1)} fusion(s32[256]{0:T(256)S(1)} %bitcast.148, f32[256]{0:T(256)S(1)} %get-tuple-element.200, f32[]{:T(128)} %constant.410.clone.1), kind=kCustom, calls=%fused_computation.648 | custom fusion | flops 256 | bytes 4100 | tf_op jit(solution)/shard_map/scatter-add | solution.py:96
  139.1 4.5 %collective-permute-start.34 = (f32[32,4,128]{2,1,0:T(4,128)S(1)}, f32[32,4,128]{2,1,0:T(4,128)S(1)}, u32[]{:S(2)}, u32[]{:S(2)}) collective-permute-start(f32[32,4,128]{2,1,0:T(4,128)S(1)} %get-tuple-element.253), channel_id=1, source_target_pairs={{0,2},{1,3},{4,6},{5,7},{8,10},{9,11},{12,14},{13,15},{16,18},{17,... | collective-permute-start | bytes 196616 | tf_op jit(solution)/shard_map/ppermute | solution.py:51
  145.2 2.3 %collective-permute-start.32 = (f32[32,16,4]{2,1,0:T(8,128)S(1)}, f32[32,16,4]{2,1,0:T(8,128)S(1)}, u32[]{:S(2)}, u32[]{:S(2)}) collective-permute-start(f32[32,16,4]{2,1,0:T(8,128)S(1)} %get-tuple-element.209), channel_id=1, source_target_pairs={{0,1},{2,3},{4,5},{6,7},{8,9},{10,11},{12,13},{14,15},{16,17},{18,... | collective-permute-start | bytes 24584 | tf_op jit(solution)/shard_map/ppermute | solution.py:51
  156.7 2.7 %fusion.339 = f32[1024]{0:T(1024)S(1)} fusion(f32[1024]{0:T(1024)S(1)} %broadcast.399.clone.4, s32[]{:T(128)} %bitcast.19, pred[1]{0:T(512)(128)(4,1)} %get-tuple-element.277, f32[1,1]{1,0:T(1,128)} %get-tuple-element.273, s32[1]{0:T(128)} %compare_select_fusion.1), kind=kLoop, calls=%fused_computation.681 | loop fusion | flops 5 | bytes 525 | tf_op jit(solution)/shard_map/scatter-add | solution.py:96
  159.7 28.4 %all-reduce.13.cloned.1.call-done = (f32[32,8,128]{2,1,0:T(8,128)}, f32[32,8,128]{2,1,0:T(8,128)}) async-done(((f32[32,8,128]{2,1,0:T(8,128)}, f32[32,8,128]{2,1,0:T(8,128)}), (f32[32,8,128]{2,1,0:T(8,128)}, f32[32,8,128]{2,1,0:T(8,128)})) %all-reduce.13.cloned.1.call-update) | async-done | bytes 262160 | tf_op jit(solution)/shard_map/psum | solution.py:130
  190.1 6.3 %pmax.7 = f32[]{:T(128)} all-reduce(f32[]{:T(128)} %abs_reduce_fusion), channel_id=1, replica_groups=mesh['groups'=2,'shots'=4,'dom'=2,'sub'=2] {'dom','sub'}, use_global_device_ids=true, to_apply=%region_7.8 | all-reduce | flops 1 | bytes 8 | tf_op jit(solution)/shard_map/pmax | solution.py:132
  197.7 3.6 %collective-permute-start.38 = (f32[32,4,128]{2,1,0:T(4,128)S(1)}, f32[32,4,128]{2,1,0:T(4,128)S(1)}, u32[]{:S(2)}, u32[]{:S(2)}) collective-permute-start(f32[32,4,128]{2,1,0:T(4,128)S(1)} %get-tuple-element.243), channel_id=1, source_target_pairs={{0,2},{1,3},{4,6},{5,7},{8,10},{9,11},{12,14},{13,15},{16,18},{17,... | collective-permute-start | bytes 196616 | tf_op jit(solution)/shard_map/ppermute | solution.py:51
  202.7 2.6 %fusion.337 = f32[1024]{0:T(1024)S(1)} fusion(f32[1024]{0:T(1024)S(1)} %broadcast.399.clone.5, s32[]{:T(128)} %bitcast.19, pred[1]{0:T(512)(128)(4,1)} %get-tuple-element.277, f32[1,1]{1,0:T(1,128)} %get-tuple-element.268, s32[1]{0:T(128)} %compare_select_fusion.1), kind=kLoop, calls=%fused_computation.678 | loop fusion | flops 5 | bytes 525 | tf_op jit(solution)/shard_map/scatter-add | solution.py:96
  (205 shorter events, 94.2 us)
Async XLA Ops:
  7.2 180.9 %all-reduce.13.cloned.1.call-start = ((), (), s32[]{:S(2)}) async-start(), calls=%async_computation | async-start | bytes 524288 | tf_op jit(solution)/shard_map/psum | solution.py:130
  8.1 34.1 %collective-permute-start.6 = (f32[32,4,128]{2,1,0:T(4,128)S(1)}, f32[32,4,128]{2,1,0:T(4,128)S(1)}, u32[]{:S(2)}, u32[]{:S(2)}) collective-permute-start(f32[32,4,128]{2,1,0:T(4,128)S(1)} %get-tuple-element.261), channel_id=1, source_target_pairs={{0,2},{1,3},{4,6},{5,7},{8,10},{9,11},{12,14},{13,15},{16,18},{17,... | collective-permute-start | bytes 196616 | tf_op jit(solution)/shard_map/ppermute | solution.py:51
  13.0 29.2 %collective-permute-start.7 = (f32[32,4,128]{2,1,0:T(4,128)S(1)}, f32[32,4,128]{2,1,0:T(4,128)S(1)}, u32[]{:S(2)}, u32[]{:S(2)}) collective-permute-start(f32[32,4,128]{2,1,0:T(4,128)S(1)} %get-tuple-element.260), channel_id=1, source_target_pairs={{2,0},{3,1},{6,4},{7,5},{10,8},{11,9},{14,12},{15,13},{18,16},{19,... | collective-permute-start | bytes 196616 | tf_op jit(solution)/shard_map/ppermute | solution.py:53
  14.3 25.2 %collective-permute-start = (f32[1,8,8,128]{3,2,1,0:T(8,128)S(1)}, f32[1,8,8,128]{3,2,1,0:T(8,128)S(1)}, u32[]{:S(2)}, u32[]{:S(2)}) collective-permute-start(f32[1,8,8,128]{3,2,1,0:T(8,128)S(1)} %bitcast.142), channel_id=1, source_target_pairs={{0,4},{4,0},{8,12},{12,8},{1,5},{5,1},{9,13},{13,9},{2,6},{6,2},{1... | collective-permute-start | bytes 98312 | tf_op jit(solution)/shard_map/ppermute | solution.py:29
  16.0 29.0 %collective-permute-start.2 = (f32[32,4,128]{2,1,0:T(4,128)S(1)}, f32[32,4,128]{2,1,0:T(4,128)S(1)}, u32[]{:S(2)}, u32[]{:S(2)}) collective-permute-start(f32[32,4,128]{2,1,0:T(4,128)S(1)} %get-tuple-element.251), channel_id=1, source_target_pairs={{0,2},{1,3},{4,6},{5,7},{8,10},{9,11},{12,14},{13,15},{16,18},{17,... | collective-permute-start | bytes 196616 | tf_op jit(solution)/shard_map/ppermute | solution.py:51
  20.6 24.5 %collective-permute-start.3 = (f32[32,4,128]{2,1,0:T(4,128)S(1)}, f32[32,4,128]{2,1,0:T(4,128)S(1)}, u32[]{:S(2)}, u32[]{:S(2)}) collective-permute-start(f32[32,4,128]{2,1,0:T(4,128)S(1)} %get-tuple-element.250), channel_id=1, source_target_pairs={{2,0},{3,1},{6,4},{7,5},{10,8},{11,9},{14,12},{15,13},{18,16},{19,... | collective-permute-start | bytes 196616 | tf_op jit(solution)/shard_map/ppermute | solution.py:53
  39.5 13.0 %collective-permute-start.1 = (f32[2,8,8,128]{3,2,1,0:T(8,128)S(1)}, f32[2,8,8,128]{3,2,1,0:T(8,128)S(1)}, u32[]{:S(2)}, u32[]{:S(2)}) collective-permute-start(f32[2,8,8,128]{3,2,1,0:T(8,128)S(1)} %get-tuple-element.263), channel_id=1, source_target_pairs={{0,8},{4,12},{8,0},{12,4},{1,9},{5,13},{9,1},{13,5},{2,10},{6,14},... | collective-permute-start | bytes 196616 | tf_op jit(solution)/shard_map/ppermute | solution.py:29
  42.4 7.2 %collective-permute-start.8 = (f32[32,16,4]{2,1,0:T(8,128)S(1)}, f32[32,16,4]{2,1,0:T(8,128)S(1)}, u32[]{:S(2)}, u32[]{:S(2)}) collective-permute-start(f32[32,16,4]{2,1,0:T(8,128)S(1)} %get-tuple-element.241), channel_id=1, source_target_pairs={{0,1},{2,3},{4,5},{6,7},{8,9},{10,11},{12,13},{14,15},{16,17},{18,... | collective-permute-start | bytes 24584 | tf_op jit(solution)/shard_map/ppermute | solution.py:51
  43.7 5.9 %collective-permute-start.9 = (f32[32,16,4]{2,1,0:T(8,128)S(1)}, f32[32,16,4]{2,1,0:T(8,128)S(1)}, u32[]{:S(2)}, u32[]{:S(2)}) collective-permute-start(f32[32,16,4]{2,1,0:T(8,128)S(1)} %get-tuple-element.240), channel_id=1, source_target_pairs={{1,0},{3,2},{5,4},{7,6},{9,8},{11,10},{13,12},{15,14},{17,16},{19,... | collective-permute-start | bytes 24584 | tf_op jit(solution)/shard_map/ppermute | solution.py:53
  54.1 6.4 %collective-permute-start.10 = (f32[32,4,128]{2,1,0:T(4,128)S(1)}, f32[32,4,128]{2,1,0:T(4,128)S(1)}, u32[]{:S(2)}, u32[]{:S(2)}) collective-permute-start(f32[32,4,128]{2,1,0:T(4,128)S(1)} %get-tuple-element.259), channel_id=1, source_target_pairs={{0,2},{1,3},{4,6},{5,7},{8,10},{9,11},{12,14},{13,15},{16,18},{17,... | collective-permute-start | bytes 196616 | tf_op jit(solution)/shard_map/ppermute | solution.py:51
  58.7 6.2 %collective-permute-start.11 = (f32[32,4,128]{2,1,0:T(4,128)S(1)}, f32[32,4,128]{2,1,0:T(4,128)S(1)}, u32[]{:S(2)}, u32[]{:S(2)}) collective-permute-start(f32[32,4,128]{2,1,0:T(4,128)S(1)} %get-tuple-element.258), channel_id=1, source_target_pairs={{2,0},{3,1},{6,4},{7,5},{10,8},{11,9},{14,12},{15,13},{18,16},{19,... | collective-permute-start | bytes 196616 | tf_op jit(solution)/shard_map/ppermute | solution.py:53
  72.8 6.2 %collective-permute-start.15 = (f32[32,4,128]{2,1,0:T(4,128)S(1)}, f32[32,4,128]{2,1,0:T(4,128)S(1)}, u32[]{:S(2)}, u32[]{:S(2)}) collective-permute-start(f32[32,4,128]{2,1,0:T(4,128)S(1)} %get-tuple-element.256), channel_id=1, source_target_pairs={{2,0},{3,1},{6,4},{7,5},{10,8},{11,9},{14,12},{15,13},{18,16},{19,... | collective-permute-start | bytes 196616 | tf_op jit(solution)/shard_map/ppermute | solution.py:53
  87.0 6.2 %collective-permute-start.19 = (f32[32,4,128]{2,1,0:T(4,128)S(1)}, f32[32,4,128]{2,1,0:T(4,128)S(1)}, u32[]{:S(2)}, u32[]{:S(2)}) collective-permute-start(f32[32,4,128]{2,1,0:T(4,128)S(1)} %get-tuple-element.254), channel_id=1, source_target_pairs={{2,0},{3,1},{6,4},{7,5},{10,8},{11,9},{14,12},{15,13},{18,16},{19,... | collective-permute-start | bytes 196616 | tf_op jit(solution)/shard_map/ppermute | solution.py:53
  105.5 6.2 %collective-permute-start.23 = (f32[32,4,128]{2,1,0:T(4,128)S(1)}, f32[32,4,128]{2,1,0:T(4,128)S(1)}, u32[]{:S(2)}, u32[]{:S(2)}) collective-permute-start(f32[32,4,128]{2,1,0:T(4,128)S(1)} %get-tuple-element.248), channel_id=1, source_target_pairs={{2,0},{3,1},{6,4},{7,5},{10,8},{11,9},{14,12},{15,13},{18,16},{19,... | collective-permute-start | bytes 196616 | tf_op jit(solution)/shard_map/ppermute | solution.py:53
  120.0 6.8 %collective-permute-start.27 = (f32[32,4,128]{2,1,0:T(4,128)S(1)}, f32[32,4,128]{2,1,0:T(4,128)S(1)}, u32[]{:S(2)}, u32[]{:S(2)}) collective-permute-start(f32[32,4,128]{2,1,0:T(4,128)S(1)} %get-tuple-element.246), channel_id=1, source_target_pairs={{2,0},{3,1},{6,4},{7,5},{10,8},{11,9},{14,12},{15,13},{18,16},{19,... | collective-permute-start | bytes 196616 | tf_op jit(solution)/shard_map/ppermute | solution.py:53
  126.9 7.9 %collective-permute-start.28 = (f32[32,16,4]{2,1,0:T(8,128)S(1)}, f32[32,16,4]{2,1,0:T(8,128)S(1)}, u32[]{:S(2)}, u32[]{:S(2)}) collective-permute-start(f32[32,16,4]{2,1,0:T(8,128)S(1)} %get-tuple-element.213), channel_id=1, source_target_pairs={{0,1},{2,3},{4,5},{6,7},{8,9},{10,11},{12,13},{14,15},{16,17},{18,... | collective-permute-start | bytes 24584 | tf_op jit(solution)/shard_map/ppermute | solution.py:51
  128.9 6.0 %collective-permute-start.29 = (f32[32,16,4]{2,1,0:T(8,128)S(1)}, f32[32,16,4]{2,1,0:T(8,128)S(1)}, u32[]{:S(2)}, u32[]{:S(2)}) collective-permute-start(f32[32,16,4]{2,1,0:T(8,128)S(1)} %get-tuple-element.212), channel_id=1, source_target_pairs={{1,0},{3,2},{5,4},{7,6},{9,8},{11,10},{13,12},{15,14},{17,16},{19,... | collective-permute-start | bytes 24584 | tf_op jit(solution)/shard_map/ppermute | solution.py:53
  136.3 8.7 %collective-permute-start.30 = (f32[32,4,128]{2,1,0:T(4,128)S(1)}, f32[32,4,128]{2,1,0:T(4,128)S(1)}, u32[]{:S(2)}, u32[]{:S(2)}) collective-permute-start(f32[32,4,128]{2,1,0:T(4,128)S(1)} %get-tuple-element.245), channel_id=1, source_target_pairs={{0,2},{1,3},{4,6},{5,7},{8,10},{9,11},{12,14},{13,15},{16,18},{17,... | collective-permute-start | bytes 196616 | tf_op jit(solution)/shard_map/ppermute | solution.py:51
  137.8 7.2 %collective-permute-start.31 = (f32[32,4,128]{2,1,0:T(4,128)S(1)}, f32[32,4,128]{2,1,0:T(4,128)S(1)}, u32[]{:S(2)}, u32[]{:S(2)}) collective-permute-start(f32[32,4,128]{2,1,0:T(4,128)S(1)} %get-tuple-element.244), channel_id=1, source_target_pairs={{2,0},{3,1},{6,4},{7,5},{10,8},{11,9},{14,12},{15,13},{18,16},{19,... | collective-permute-start | bytes 196616 | tf_op jit(solution)/shard_map/ppermute | solution.py:53
  139.1 9.9 %collective-permute-start.34 = (f32[32,4,128]{2,1,0:T(4,128)S(1)}, f32[32,4,128]{2,1,0:T(4,128)S(1)}, u32[]{:S(2)}, u32[]{:S(2)}) collective-permute-start(f32[32,4,128]{2,1,0:T(4,128)S(1)} %get-tuple-element.253), channel_id=1, source_target_pairs={{0,2},{1,3},{4,6},{5,7},{8,10},{9,11},{12,14},{13,15},{16,18},{17,... | collective-permute-start | bytes 196616 | tf_op jit(solution)/shard_map/ppermute | solution.py:51
  143.7 6.3 %collective-permute-start.35 = (f32[32,4,128]{2,1,0:T(4,128)S(1)}, f32[32,4,128]{2,1,0:T(4,128)S(1)}, u32[]{:S(2)}, u32[]{:S(2)}) collective-permute-start(f32[32,4,128]{2,1,0:T(4,128)S(1)} %get-tuple-element.252), channel_id=1, source_target_pairs={{2,0},{3,1},{6,4},{7,5},{10,8},{11,9},{14,12},{15,13},{18,16},{19,... | collective-permute-start | bytes 196616 | tf_op jit(solution)/shard_map/ppermute | solution.py:53
  153.3 6.0 %collective-permute-start.36 = (f32[32,16,4]{2,1,0:T(8,128)S(1)}, f32[32,16,4]{2,1,0:T(8,128)S(1)}, u32[]{:S(2)}, u32[]{:S(2)}) collective-permute-start(f32[32,16,4]{2,1,0:T(8,128)S(1)} %get-tuple-element.225), channel_id=1, source_target_pairs={{0,1},{2,3},{4,5},{6,7},{8,9},{10,11},{12,13},{14,15},{16,17},{18,... | collective-permute-start | bytes 24584 | tf_op jit(solution)/shard_map/ppermute | solution.py:51
  197.7 7.5 %collective-permute-start.38 = (f32[32,4,128]{2,1,0:T(4,128)S(1)}, f32[32,4,128]{2,1,0:T(4,128)S(1)}, u32[]{:S(2)}, u32[]{:S(2)}) collective-permute-start(f32[32,4,128]{2,1,0:T(4,128)S(1)} %get-tuple-element.243), channel_id=1, source_target_pairs={{0,2},{1,3},{4,6},{5,7},{8,10},{9,11},{12,14},{13,15},{16,18},{17,... | collective-permute-start | bytes 196616 | tf_op jit(solution)/shard_map/ppermute | solution.py:51
  201.4 6.2 %collective-permute-start.39 = (f32[32,4,128]{2,1,0:T(4,128)S(1)}, f32[32,4,128]{2,1,0:T(4,128)S(1)}, u32[]{:S(2)}, u32[]{:S(2)}) collective-permute-start(f32[32,4,128]{2,1,0:T(4,128)S(1)} %get-tuple-element.242), channel_id=1, source_target_pairs={{2,0},{3,1},{6,4},{7,5},{10,8},{11,9},{14,12},{15,13},{18,16},{19,... | collective-permute-start | bytes 196616 | tf_op jit(solution)/shard_map/ppermute | solution.py:53
  (30 other events, 109.1 us)
Sparse Core Ops, SparseCore 0:
  153.3 34.7 all-reduce.12
